TPU v7x, 512 devices: a whole 4x8x8 slice. The times are simulated.
512 devices in a mesh: span: 16 (over z_hi, x), wall: 16 (over y, core), stream: 2 (over z_lo).
Axes of the slice: x: 4, y: 8, z: 8 (z_hi: 4, z_lo: 2; z = z_hi * 2 + z_lo), core: 2. Of those that a mesh axis runs over, the one named last changes fastest.
Arguments:
- fields: float32 [4, 16, 256, 2048], P(None, 'stream', 'wall', 'span'), may hold values from -67.5 to 67.5, as said below
Outputs:
- clark_model: float32 [3, 16, 256, 2048], P(None, 'stream', 'wall', 'span')
- similar_model: float32 [3, 16, 256, 2048], P(None, 'stream', 'wall', 'span')
- clark_corr: float32 [3, 256], P(None, 'wall')
- similar_corr: float32 [3, 256], P(None, 'wall')
Inputs may be any that keep to these rules, and one draw needn't show every extreme that they name: The fields are rough from cell to cell.
All inputs are finite; a program needn't handle non-finite values.
Results may differ from a plain program's by a relative error of at most 0.00024.
Values sent between devices are 32-bit elements; how exact they have to be, the bound alone decides.
A program may use at most 64 MiB of HBM per device.

v0:
```python
import math
import jax
import jax.numpy as jnp
from jax import lax
from jax.sharding import PartitionSpec as P

raw_taps = [math.exp(-((k - 8) ** 2) / 18.0) for k in range(17)]
filter_taps = [value / sum(raw_taps) for value in raw_taps]
clark_coef = 9.0
small_eps = 1e-06


def with_halo(cells, sides, width, closed):
    for axis, dim in sides:
        count = lax.axis_size(axis)
        ends = count if closed else count - 1
        head = lax.slice_in_dim(cells, 0, width, axis=dim)
        tail = lax.slice_in_dim(cells, cells.shape[dim] - width, cells.shape[dim], axis=dim)
        cells = jnp.concatenate(
            [
                lax.ppermute(tail, axis, [(i, (i + 1) % count) for i in range(ends)]),
                cells,
                lax.ppermute(head, axis, [((i + 1) % count, i) for i in range(ends)]),
            ],
            axis=dim,
        )
    return cells


def band_matrix(length):
    offset = (
        jnp.arange(length + 16, dtype=jnp.int32)[:, None]
        - jnp.arange(length, dtype=jnp.int32)[None, :]
    )
    matrix = jnp.zeros((length + 16, length), jnp.float32)
    for k in range(17):
        matrix = matrix + jnp.where(offset == k, filter_taps[k], 0.0).astype(jnp.float32)
    return matrix


def smooth(padded, direction, length):
    matrix = band_matrix(length)
    if direction == 3:
        return jnp.einsum("fswz,zk->fswk", padded, matrix, precision=lax.Precision.HIGHEST)
    if direction == 2:
        return jnp.einsum("fswz,wk->fskz", padded, matrix, precision=lax.Precision.HIGHEST)
    return jnp.einsum("fswz,sk->fkwz", padded, matrix, precision=lax.Precision.HIGHEST)


def with_products(quad):
    return jnp.concatenate([quad, quad[:3] * quad[3:4]], axis=0)


def filter_all(quad):
    stream_len, wall_len, span_len = (quad.shape[1], quad.shape[2], quad.shape[3])
    payload = with_products(quad)
    spanned = with_halo(payload, (("span", 3),), 8, True)
    extended = with_halo(spanned, (("wall", 2), ("stream", 1)), 8, False)
    kept = extended[:4]
    result = smooth(extended, 3, span_len)
    result = smooth(result, 2, wall_len)
    return (smooth(result, 1, stream_len), kept)


def clark_flux(means):
    padded = with_halo(means, (("span", 3),), 1, True)
    along_span = (padded[..., 2:] - padded[..., :-2]) * 0.5
    plane = with_halo(means, (("wall", 2), ("stream", 1)), 1, False)
    along_wall = (plane[:, 1:-1, 2:, :] - plane[:, 1:-1, :-2, :]) * 0.5
    along_stream = (plane[:, 2:, 1:-1, :] - plane[:, :-2, 1:-1, :]) * 0.5
    total = along_span[:3] * along_span[3:4] + along_wall[:3] * along_wall[3:4]
    total = total + along_stream[:3] * along_stream[3:4]
    return clark_coef * total


def shards(fields):
    first, unused_rim = filter_all(fields)
    means = first[:4]
    exact = first[4:] - means[:3] * means[3:4]
    second, mean_rim = filter_all(means)
    similar = second[4:] - second[:3] * second[3:4]
    clark = clark_flux(means)
    sums = (
        jnp.sum(exact * clark, axis=(1, 3)),
        jnp.sum(exact * similar, axis=(1, 3)),
        jnp.sum(exact * exact, axis=(1, 3)),
        jnp.sum(clark * clark, axis=(1, 3)),
        jnp.sum(similar * similar, axis=(1, 3)),
    )
    cross_c, cross_s, power_e, power_c, power_s = lax.psum(
        (sums[0], sums[1], sums[2], sums[3], sums[4]), ("span", "stream")
    )
    plane_cells = float(
        fields.shape[1] * fields.shape[3] * lax.axis_size("stream") * lax.axis_size("span")
    )
    cross_c = cross_c / plane_cells
    cross_s = cross_s / plane_cells
    power_e = power_e / plane_cells
    power_c = power_c / plane_cells
    power_s = power_s / plane_cells
    clark_corr = cross_c / jnp.sqrt((power_e + small_eps) * (power_c + small_eps))
    similar_corr = cross_s / jnp.sqrt((power_e + small_eps) * (power_s + small_eps))
    clark_model = clark / jnp.sqrt(power_c + small_eps)[:, None, :, None]
    similar_model = similar / jnp.sqrt(power_s + small_eps)[:, None, :, None]
    return (clark_model, similar_model, clark_corr, similar_corr)


def solution(mesh):
    return jax.shard_map(
        shards,
        mesh=mesh,
        in_specs=(P(None, "stream", "wall", "span"),),
        out_specs=(
            P(None, "stream", "wall", "span"),
            P(None, "stream", "wall", "span"),
            P(None, "wall"),
            P(None, "wall"),
        ),
        check_vma=False,
    )
```

profile of v0, /device:TPU:16, one launch (start us, length us, event | category | flops | bytes accessed | tf_op | source)
XLA Modules:
  0.0 371.7 jit_solution(2666519787292298506)
XLA Ops:
  0.6 0.8 slice_bitcast_fusion.5
  1.5 0.9 slice_multiply_fusion.5
  2.4 1.3 slice_maximum_fusion.1
  3.7 13.1 %collective-permute-start.1 = (f32[7,8,16,8]{3,2,1,0:T(8,128)S(1)}, f32[7,8,16,8]{3,2,1,0:T(8,128)S(1)}, u32[]{:S(2)}, u32[]{:S(2)}) collective-permute-start(f32[7,8,16,8]{3,2,1,0:T(8,128)S(1)} %get-tuple-element.31), channel_id=1, source_target_pairs={{32,0},{64,32},{96,64},{128,96},{160,128},{192,160},{224,192},{256... | collective-permute-start | bytes 86024 | tf_op jit(solution)/shard_map/ppermute | solution.py:23
  16.9 1.9 collective-permute-start
  18.8 17.7 %collective-permute-done.1 = f32[7,8,16,8]{3,2,1,0:T(8,128)S(1)} collective-permute-done((f32[7,8,16,8]{3,2,1,0:T(8,128)S(1)}, f32[7,8,16,8]{3,2,1,0:T(8,128)S(1)}, u32[]{:S(2)}, u32[]{:S(2)}) %collective-permute-start.1) | collective-permute-done | bytes 28704 | tf_op jit(solution)/shard_map/ppermute | solution.py:23
  36.4 8.3 %collective-permute-done = f32[7,8,16,8]{3,2,1,0:T(8,128)S(1)} collective-permute-done((f32[7,8,16,8]{3,2,1,0:T(8,128)S(1)}, f32[7,8,16,8]{3,2,1,0:T(8,128)S(1)}, u32[]{:S(2)}, u32[]{:S(2)}) %collective-permute-start) | collective-permute-done | bytes 28704 | tf_op jit(solution)/shard_map/ppermute | solution.py:21
  44.8 1.4 pad_maximum_fusion.3
  46.3 1.9 collective-permute-start.3
  48.2 2.4 collective-permute-start.2
  50.6 3.6 collective-permute-done.3
  54.2 3.8 %collective-permute-done.2 = f32[7,8,8,144]{3,2,1,0:T(8,128)S(1)} collective-permute-done((f32[7,8,8,144]{3,2,1,0:T(8,128)S(1)}, f32[7,8,8,144]{3,2,1,0:T(8,128)S(1)}, u32[]{:S(2)}, u32[]{:S(2)}) %collective-permute-start.2) | collective-permute-done | bytes 258080 | tf_op jit(solution)/shard_map/ppermute | solution.py:21
  58.5 1.3 collective-permute-start.5
  59.8 4.8 %collective-permute-start.4 = (f32[7,8,32,144]{3,2,1,0:T(8,128)S(1)}, f32[7,8,32,144]{3,2,1,0:T(8,128)S(1)}, u32[]{:S(2)}, u32[]{:S(2)}) collective-permute-start(f32[7,8,32,144]{3,2,1,0:T(8,128)S(1)} %pad_maximum_fusion.1), channel_id=1, source_target_pairs={{0,1},{2,3},{4,5},{6,7},{8,9},{10,11},{12,13},{14,15},{16,17},{18,... | collective-permute-start | bytes 3096584 | tf_op jit(solution)/shard_map/ppermute | solution.py:21
  64.5 36.9 %collective-permute-done.5 = f32[7,8,32,144]{3,2,1,0:T(8,128)S(1)} collective-permute-done((f32[7,8,32,144]{3,2,1,0:T(8,128)S(1)}, f32[7,8,32,144]{3,2,1,0:T(8,128)S(1)}, u32[]{:S(2)}, u32[]{:S(2)}) %collective-permute-start.5) | collective-permute-done | bytes 1032224 | tf_op jit(solution)/shard_map/ppermute | solution.py:23
  101.5 1.3 collective-permute-done.4
  102.8 4.7 %fusion = f32[7,24,32,128]{3,2,1,0:T(8,128)S(1)} fusion(f32[7,8,32,144]{3,2,1,0:T(8,128)S(1)} %collective-permute-done.5, f32[7,8,8,144]{3,2,1,0:T(8,128)S(1)} %collective-permute-done.3, f32[7,8,16,8]{3,2,1,0:T(8,128)S(1)} %collective-permute-done.1, f32[3,8,16,128]{3,2,1,0:T(8,128)S(1)} %slice_multiply_fusion.5, f32[4,8,16,128]{3,2,1,0:T(8,128)S(1)} %copy-done, ...), kind=kOutput, calls=%fused_computation | convolution fusion | flops 1195444224 | bytes 5849088 | tf_op jit(solution)/shard_map/fswz,zk->fswk/dot_general | solution.py:44
  107.5 1.5 fusion.61
  109.0 1.2 fusion.24
  110.5 1.9 collective-permute-start.13
  112.4 3.9 %collective-permute-start.12 = (f32[7,8,16,8]{3,1,2,0:T(8,128)S(1)}, f32[7,8,16,8]{3,1,2,0:T(8,128)S(1)}, u32[]{:S(2)}, u32[]{:S(2)}) collective-permute-start(f32[7,8,16,8]{3,1,2,0:T(8,128)S(1)} %get-tuple-element.28), channel_id=1, source_target_pairs={{0,32},{32,64},{64,96},{96,128},{128,160},{160,192},{192,224},{224... | collective-permute-start | bytes 86024 | tf_op jit(solution)/shard_map/ppermute | solution.py:21
  116.3 14.1 %collective-permute-done.13 = f32[7,8,16,8]{3,1,2,0:T(8,128)S(1)} collective-permute-done((f32[7,8,16,8]{3,1,2,0:T(8,128)S(1)}, f32[7,8,16,8]{3,1,2,0:T(8,128)S(1)}, u32[]{:S(2)}, u32[]{:S(2)}) %collective-permute-start.13) | collective-permute-done | bytes 28704 | tf_op jit(solution)/shard_map/ppermute | solution.py:23
  130.4 8.3 %collective-permute-done.12 = f32[7,8,16,8]{3,1,2,0:T(8,128)S(1)} collective-permute-done((f32[7,8,16,8]{3,1,2,0:T(8,128)S(1)}, f32[7,8,16,8]{3,1,2,0:T(8,128)S(1)}, u32[]{:S(2)}, u32[]{:S(2)}) %collective-permute-start.12) | collective-permute-done | bytes 28704 | tf_op jit(solution)/shard_map/ppermute | solution.py:21
  139.3 1.9 collective-permute-start.15
  141.2 2.4 collective-permute-start.14
  143.6 3.6 collective-permute-done.15
  147.2 3.8 %collective-permute-done.14 = f32[7,8,8,144]{3,1,2,0:T(8,128)S(1)} collective-permute-done((f32[7,8,8,144]{3,1,2,0:T(8,128)S(1)}, f32[7,8,8,144]{3,1,2,0:T(8,128)S(1)}, u32[]{:S(2)}, u32[]{:S(2)}) %collective-permute-start.14) | collective-permute-done | bytes 258080 | tf_op jit(solution)/shard_map/ppermute | solution.py:21
  151.0 0.4 pad_maximum_fusion.2
  151.4 1.3 collective-permute-start.17
  152.7 4.8 %collective-permute-start.16 = (f32[7,8,32,144]{3,1,2,0:T(8,128)S(1)}, f32[7,8,32,144]{3,1,2,0:T(8,128)S(1)}, u32[]{:S(2)}, u32[]{:S(2)}) collective-permute-start(f32[7,8,32,144]{3,1,2,0:T(8,128)S(1)} %pad_maximum_fusion.2), channel_id=1, source_target_pairs={{0,1},{2,3},{4,5},{6,7},{8,9},{10,11},{12,13},{14,15},{16,17},{18,... | collective-permute-start | bytes 3096584 | tf_op jit(solution)/shard_map/ppermute | solution.py:21
  157.5 3.3 collective-permute-start.9
  160.8 2.5 collective-permute-start.8
  163.3 3.1 collective-permute-done.8
  166.5 1.3 collective-permute-start.11
  167.8 1.3 collective-permute-start.10
  169.2 1.9 collective-permute-start.7
  171.2 38.2 %collective-permute-done.7 = f32[4,8,16,1]{3,1,2,0:T(8,128)S(1)} collective-permute-done((f32[4,8,16,1]{3,1,2,0:T(8,128)S(1)}, f32[4,8,16,1]{3,1,2,0:T(8,128)S(1)}, u32[]{:S(2)}, u32[]{:S(2)}) %collective-permute-start.7) | collective-permute-done | bytes 2080 | tf_op jit(solution)/shard_map/ppermute | solution.py:21
  209.3 1.9 collective-permute-start.6
  211.2 8.4 %collective-permute-done.6 = f32[4,8,16,1]{3,1,2,0:T(8,128)S(1)} collective-permute-done((f32[4,8,16,1]{3,1,2,0:T(8,128)S(1)}, f32[4,8,16,1]{3,1,2,0:T(8,128)S(1)}, u32[]{:S(2)}, u32[]{:S(2)}) %collective-permute-start.6) | collective-permute-done | bytes 2080 | tf_op jit(solution)/shard_map/ppermute | solution.py:23
  220.1 2.6 pad_maximum_fusion
  222.7 5.8 %fusion.16 = f32[7,24,32,128]{3,2,1,0:T(8,128)S(1)} fusion(f32[7,24,32,144]{3,1,2,0:T(8,128)S(1)} %pad_maximum_fusion), kind=kOutput, calls=%fused_computation.17 | convolution fusion | flops 1190025216 | bytes 5849088 | tf_op jit(solution)/shard_map/fswz,zk->fswk/dot_general | solution.py:44
  228.5 1.5 fusion.59
  230.0 1.2 fusion.27
  231.2 0.5 multiply_reduce_fusion
  231.8 137.7 %all-reduce = (f32[3,16]{1,0:T(4,128)S(1)}, f32[3,16]{1,0:T(4,128)S(1)}, f32[3,16]{1,0:T(4,128)S(1)}, f32[3,16]{1,0:T(4,128)S(1)}, f32[3,16]{1,0:T(4,128)S(1)}) all-reduce(f32[3,16]{1,0:T(4,128)S(1)} %get-tuple-element.11, f32[3,16]{1,0:T(4,128)S(1)} %get-tuple-element.12, ...), channel_id=1, replica_groups=mesh['span'=16,'wall'=16,'stream'=2] {'span','stream'}, use_global_device_ids=true, to_apply=%region_1.2 | all-reduce | flops 240 | bytes 1920 | tf_op jit(solution)/shard_map/psum | solution.py:90
  369.5 0.6 rsqrt_multiply_fusion
  370.2 0.7 copy.5
  371.0 0.7 copy.6
  (24 shorter events, 2.0 us)
Async XLA Ops:
  2.4 55.6 %copy-start = (f32[4,8,16,128]{3,2,1,0:T(8,128)S(1)}, f32[4,8,16,128]{3,2,1,0:T(8,128)}, u32[]{:S(2)}) copy-start(f32[4,8,16,128]{3,2,1,0:T(8,128)} %param.1) | copy-start | bytes 786436
  3.7 32.7 %collective-permute-start.1 = (f32[7,8,16,8]{3,2,1,0:T(8,128)S(1)}, f32[7,8,16,8]{3,2,1,0:T(8,128)S(1)}, u32[]{:S(2)}, u32[]{:S(2)}) collective-permute-start(f32[7,8,16,8]{3,2,1,0:T(8,128)S(1)} %get-tuple-element.31), channel_id=1, source_target_pairs={{32,0},{64,32},{96,64},{128,96},{160,128},{192,160},{224,192},{256... | collective-permute-start | bytes 86024 | tf_op jit(solution)/shard_map/ppermute | solution.py:23
  16.9 27.9 %collective-permute-start = (f32[7,8,16,8]{3,2,1,0:T(8,128)S(1)}, f32[7,8,16,8]{3,2,1,0:T(8,128)S(1)}, u32[]{:S(2)}, u32[]{:S(2)}) collective-permute-start(f32[7,8,16,8]{3,2,1,0:T(8,128)S(1)} %get-tuple-element.30), channel_id=1, source_target_pairs={{0,32},{32,64},{64,96},{96,128},{128,160},{160,192},{192,224},{224... | collective-permute-start | bytes 86024 | tf_op jit(solution)/shard_map/ppermute | solution.py:21
  46.3 7.9 %collective-permute-start.3 = (f32[7,8,8,144]{3,2,1,0:T(8,128)S(1)}, f32[7,8,8,144]{3,2,1,0:T(8,128)S(1)}, u32[]{:S(2)}, u32[]{:S(2)}) collective-permute-start(f32[7,8,8,144]{3,2,1,0:T(8,128)S(1)} %get-tuple-element.23), channel_id=1, source_target_pairs={{2,0},{4,2},{6,4},{8,6},{10,8},{12,10},{14,12},{16,14},{18,16},{20... | collective-permute-start | bytes 774152 | tf_op jit(solution)/shard_map/ppermute | solution.py:23
  48.2 9.8 %collective-permute-start.2 = (f32[7,8,8,144]{3,2,1,0:T(8,128)S(1)}, f32[7,8,8,144]{3,2,1,0:T(8,128)S(1)}, u32[]{:S(2)}, u32[]{:S(2)}) collective-permute-start(f32[7,8,8,144]{3,2,1,0:T(8,128)S(1)} %get-tuple-element.22), channel_id=1, source_target_pairs={{0,2},{2,4},{4,6},{6,8},{8,10},{10,12},{12,14},{14,16},{16,18},{18... | collective-permute-start | bytes 774152 | tf_op jit(solution)/shard_map/ppermute | solution.py:21
  58.5 43.0 %collective-permute-start.5 = (f32[7,8,32,144]{3,2,1,0:T(8,128)S(1)}, f32[7,8,32,144]{3,2,1,0:T(8,128)S(1)}, u32[]{:S(2)}, u32[]{:S(2)}) collective-permute-start(f32[7,8,32,144]{3,2,1,0:T(8,128)S(1)} %pad_maximum_fusion.1), channel_id=1, source_target_pairs={{1,0},{3,2},{5,4},{7,6},{9,8},{11,10},{13,12},{15,14},{17,16},{19,... | collective-permute-start | bytes 3096584 | tf_op jit(solution)/shard_map/ppermute | solution.py:23
  59.8 43.0 %collective-permute-start.4 = (f32[7,8,32,144]{3,2,1,0:T(8,128)S(1)}, f32[7,8,32,144]{3,2,1,0:T(8,128)S(1)}, u32[]{:S(2)}, u32[]{:S(2)}) collective-permute-start(f32[7,8,32,144]{3,2,1,0:T(8,128)S(1)} %pad_maximum_fusion.1), channel_id=1, source_target_pairs={{0,1},{2,3},{4,5},{6,7},{8,9},{10,11},{12,13},{14,15},{16,17},{18,... | collective-permute-start | bytes 3096584 | tf_op jit(solution)/shard_map/ppermute | solution.py:21
  110.5 20.0 %collective-permute-start.13 = (f32[7,8,16,8]{3,1,2,0:T(8,128)S(1)}, f32[7,8,16,8]{3,1,2,0:T(8,128)S(1)}, u32[]{:S(2)}, u32[]{:S(2)}) collective-permute-start(f32[7,8,16,8]{3,1,2,0:T(8,128)S(1)} %get-tuple-element.29), channel_id=1, source_target_pairs={{32,0},{64,32},{96,64},{128,96},{160,128},{192,160},{224,192},{256... | collective-permute-start | bytes 86024 | tf_op jit(solution)/shard_map/ppermute | solution.py:23
  112.4 26.4 %collective-permute-start.12 = (f32[7,8,16,8]{3,1,2,0:T(8,128)S(1)}, f32[7,8,16,8]{3,1,2,0:T(8,128)S(1)}, u32[]{:S(2)}, u32[]{:S(2)}) collective-permute-start(f32[7,8,16,8]{3,1,2,0:T(8,128)S(1)} %get-tuple-element.28), channel_id=1, source_target_pairs={{0,32},{32,64},{64,96},{96,128},{128,160},{160,192},{192,224},{224... | collective-permute-start | bytes 86024 | tf_op jit(solution)/shard_map/ppermute | solution.py:21
  139.3 7.9 %collective-permute-start.15 = (f32[7,8,8,144]{3,1,2,0:T(8,128)S(1)}, f32[7,8,8,144]{3,1,2,0:T(8,128)S(1)}, u32[]{:S(2)}, u32[]{:S(2)}) collective-permute-start(f32[7,8,8,144]{3,1,2,0:T(8,128)S(1)} %get-tuple-element.21), channel_id=1, source_target_pairs={{2,0},{4,2},{6,4},{8,6},{10,8},{12,10},{14,12},{16,14},{18,16},{20... | collective-permute-start | bytes 774152 | tf_op jit(solution)/shard_map/ppermute | solution.py:23
  141.2 9.8 %collective-permute-start.14 = (f32[7,8,8,144]{3,1,2,0:T(8,128)S(1)}, f32[7,8,8,144]{3,1,2,0:T(8,128)S(1)}, u32[]{:S(2)}, u32[]{:S(2)}) collective-permute-start(f32[7,8,8,144]{3,1,2,0:T(8,128)S(1)} %get-tuple-element.20), channel_id=1, source_target_pairs={{0,2},{2,4},{4,6},{6,8},{8,10},{10,12},{12,14},{14,16},{16,18},{18... | collective-permute-start | bytes 774152 | tf_op jit(solution)/shard_map/ppermute | solution.py:21
  151.4 68.6 %collective-permute-start.17 = (f32[7,8,32,144]{3,1,2,0:T(8,128)S(1)}, f32[7,8,32,144]{3,1,2,0:T(8,128)S(1)}, u32[]{:S(2)}, u32[]{:S(2)}) collective-permute-start(f32[7,8,32,144]{3,1,2,0:T(8,128)S(1)} %pad_maximum_fusion.2), channel_id=1, source_target_pairs={{1,0},{3,2},{5,4},{7,6},{9,8},{11,10},{13,12},{15,14},{17,16},{19,... | collective-permute-start | bytes 3096584 | tf_op jit(solution)/shard_map/ppermute | solution.py:23
  152.7 67.3 %collective-permute-start.16 = (f32[7,8,32,144]{3,1,2,0:T(8,128)S(1)}, f32[7,8,32,144]{3,1,2,0:T(8,128)S(1)}, u32[]{:S(2)}, u32[]{:S(2)}) collective-permute-start(f32[7,8,32,144]{3,1,2,0:T(8,128)S(1)} %pad_maximum_fusion.2), channel_id=1, source_target_pairs={{0,1},{2,3},{4,5},{6,7},{8,9},{10,11},{12,13},{14,15},{16,17},{18,... | collective-permute-start | bytes 3096584 | tf_op jit(solution)/shard_map/ppermute | solution.py:21
  157.5 5.8 %collective-permute-start.9 = (f32[4,8,1,128]{3,1,2,0:T(8,128)S(1)}, f32[4,8,1,128]{3,1,2,0:T(8,128)S(1)}, u32[]{:S(2)}, u32[]{:S(2)}) collective-permute-start(f32[4,8,1,128]{3,1,2,0:T(8,128)S(1)} %get-tuple-element.26), channel_id=1, source_target_pairs={{0,2},{2,4},{4,6},{6,8},{8,10},{10,12},{12,14},{14,16},{16,18},{18... | collective-permute-start | bytes 49160 | tf_op jit(solution)/shard_map/ppermute | solution.py:21
  160.8 5.6 %collective-permute-start.8 = (f32[4,8,1,128]{3,1,2,0:T(8,128)S(1)}, f32[4,8,1,128]{3,1,2,0:T(8,128)S(1)}, u32[]{:S(2)}, u32[]{:S(2)}) collective-permute-start(f32[4,8,1,128]{3,1,2,0:T(8,128)S(1)} %get-tuple-element.27), channel_id=1, source_target_pairs={{2,0},{4,2},{6,4},{8,6},{10,8},{12,10},{14,12},{16,14},{18,16},{20... | collective-permute-start | bytes 49160 | tf_op jit(solution)/shard_map/ppermute | solution.py:23
  166.5 53.2 %collective-permute-start.11 = (f32[4,1,18,128]{3,1,2,0:T(1,128)S(1)}, f32[4,1,18,128]{3,1,2,0:T(1,128)S(1)}, u32[]{:S(2)}, u32[]{:S(2)}) collective-permute-start(f32[4,1,18,128]{3,1,2,0:T(1,128)S(1)} %get-tuple-element.35), channel_id=1, source_target_pairs={{0,1},{2,3},{4,5},{6,7},{8,9},{10,11},{12,13},{14,15},{16,17},{18,... | collective-permute-start | bytes 110600 | tf_op jit(solution)/shard_map/ppermute | solution.py:21
  167.8 51.9 %collective-permute-start.10 = (f32[4,1,18,128]{3,1,2,0:T(1,128)S(1)}, f32[4,1,18,128]{3,1,2,0:T(1,128)S(1)}, u32[]{:S(2)}, u32[]{:S(2)}) collective-permute-start(f32[4,1,18,128]{3,1,2,0:T(1,128)S(1)} %get-tuple-element.34), channel_id=1, source_target_pairs={{1,0},{3,2},{5,4},{7,6},{9,8},{11,10},{13,12},{15,14},{17,16},{19,... | collective-permute-start | bytes 110600 | tf_op jit(solution)/shard_map/ppermute | solution.py:23
  169.2 40.1 %collective-permute-start.7 = (f32[4,8,16,1]{3,1,2,0:T(8,128)S(1)}, f32[4,8,16,1]{3,1,2,0:T(8,128)S(1)}, u32[]{:S(2)}, u32[]{:S(2)}) collective-permute-start(f32[4,8,16,1]{3,1,2,0:T(8,128)S(1)} %get-tuple-element.25), channel_id=1, source_target_pairs={{0,32},{32,64},{64,96},{96,128},{128,160},{160,192},{192,224},{224... | collective-permute-start | bytes 6152 | tf_op jit(solution)/shard_map/ppermute | solution.py:21
  209.3 10.3 %collective-permute-start.6 = (f32[4,8,16,1]{3,1,2,0:T(8,128)S(1)}, f32[4,8,16,1]{3,1,2,0:T(8,128)S(1)}, u32[]{:S(2)}, u32[]{:S(2)}) collective-permute-start(f32[4,8,16,1]{3,1,2,0:T(8,128)S(1)} %get-tuple-element.24), channel_id=1, source_target_pairs={{32,0},{64,32},{96,64},{128,96},{160,128},{192,160},{224,192},{256... | collective-permute-start | bytes 6152 | tf_op jit(solution)/shard_map/ppermute | solution.py:23
where the time goes:
time: 372 us
  waiting for transfers between devices  151 us (41%)
  blocking collectives  138 us (37%)
  starting transfers between devices  53.8 us (14%)
  matrix products  15.9 us (4%)
  other arithmetic  9.48 us (3%)
    psum x1, blocking collectives, shards(): lax.psum((sums[0], sums[1], sums[2], sums[3], sums[4]), ('span', 'stream'))  138 us
    ppermute x9, waiting for transfers between devices, with_halo(): lax.ppermute(head, axis, [((i + 1) % count, i) for i in range(ends)])  87.4 us
    ppermute x9, waiting for transfers between devices, with_halo(): lax.ppermute(tail, axis, [(i, (i + 1) % count) for i in range(ends)])  63.8 us
    ppermute x9, starting transfers between devices, with_halo(): lax.ppermute(head, axis, [((i + 1) % count, i) for i in range(ends)])  27.1 us
    ppermute x9, starting transfers between devices, with_halo(): lax.ppermute(tail, axis, [(i, (i + 1) % count) for i in range(ends)])  26.7 us
    dot_general x2, matrix products, smooth(): jnp.einsum('fswz,zk->fswk', padded, matrix, precision=lax.Precision.HIGHEST)  10.5 us
  transfers between devices with their start and end apart: 18, of which 13 were waited for; matrix products, arithmetic and copies ran while one was open for 0% of the time, Pallas kernels for 0%

commit v1 on v0

--- a/solution.py
+++ b/solution.py
@@ -88,7 +88,7 @@
         jnp.sum(similar * similar, axis=(1, 3)),
     )
     cross_c, cross_s, power_e, power_c, power_s = lax.psum(
-        (sums[0], sums[1], sums[2], sums[3], sums[4]), ("span", "stream")
+        lax.psum((sums[0], sums[1], sums[2], sums[3], sums[4]), "span"), "stream"
     )
     plane_cells = float(
         fields.shape[1] * fields.shape[3] * lax.axis_size("stream") * lax.axis_size("span")

time: 372 us -> 323 us (0.87)
  blocking collectives: 138 us -> 87.9 us
    psum x1 -> x2, blocking collectives: 138 us -> 87.9 us  [the longest x1 81.2 us: shards(): lax.psum((sums[0], sums[1], sums[2], sums[3], sums[4]), 'span')]
where the time goes in v1:
time: 323 us; the launch traced here: 322 us
  waiting for transfers between devices  151 us (47%)
  blocking collectives  87.9 us (27%)
  starting transfers between devices  53.8 us (17%)
  matrix products  15.9 us (5%)
  other arithmetic  9.49 us (3%)
    ppermute x9, waiting for transfers between devices, with_halo(): lax.ppermute(head, axis, [((i + 1) % count, i) for i in range(ends)])  87.4 us
    psum x1, blocking collectives, shards(): lax.psum((sums[0], sums[1], sums[2], sums[3], sums[4]), 'span')  81.2 us
    ppermute x9, waiting for transfers between devices, with_halo(): lax.ppermute(tail, axis, [(i, (i + 1) % count) for i in range(ends)])  63.8 us
    ppermute x9, starting transfers between devices, with_halo(): lax.ppermute(head, axis, [((i + 1) % count, i) for i in range(ends)])  27.1 us
    ppermute x9, starting transfers between devices, with_halo(): lax.ppermute(tail, axis, [(i, (i + 1) % count) for i in range(ends)])  26.7 us
    dot_general x2, matrix products, smooth(): jnp.einsum('fswz,zk->fswk', padded, matrix, precision=lax.Precision.HIGHEST)  10.5 us
    psum x1, blocking collectives, shards(): lax.psum(lax.psum((sums[0], sums[1], sums[2], sums[3], sums[4]), 'span'),...  6.69 us
  transfers between devices with their start and end apart: 18, of which 13 were waited for; matrix products, arithmetic and copies ran while one was open for 0% of the time, Pallas kernels for 0%

profile of v1, /device:TPU:16, one launch (start us, length us, event | category | flops | bytes accessed | tf_op | source)
XLA Modules:
  0.0 322.0 jit_solution(12657176683517413170)
XLA Ops:
  0.6 0.8 slice_bitcast_fusion.5
  1.5 0.9 slice_multiply_fusion.5
  2.4 1.3 slice_maximum_fusion.1
  3.7 13.1 %collective-permute-start.1 = (f32[7,8,16,8]{3,2,1,0:T(8,128)S(1)}, f32[7,8,16,8]{3,2,1,0:T(8,128)S(1)}, u32[]{:S(2)}, u32[]{:S(2)}) collective-permute-start(f32[7,8,16,8]{3,2,1,0:T(8,128)S(1)} %get-tuple-element.36), channel_id=1, source_target_pairs={{32,0},{64,32},{96,64},{128,96},{160,128},{192,160},{224,192},{256... | collective-permute-start | bytes 86024 | tf_op jit(solution)/shard_map/ppermute | solution.py:23
  16.9 1.9 collective-permute-start
  18.8 17.7 %collective-permute-done.1 = f32[7,8,16,8]{3,2,1,0:T(8,128)S(1)} collective-permute-done((f32[7,8,16,8]{3,2,1,0:T(8,128)S(1)}, f32[7,8,16,8]{3,2,1,0:T(8,128)S(1)}, u32[]{:S(2)}, u32[]{:S(2)}) %collective-permute-start.1) | collective-permute-done | bytes 28704 | tf_op jit(solution)/shard_map/ppermute | solution.py:23
  36.4 8.3 %collective-permute-done = f32[7,8,16,8]{3,2,1,0:T(8,128)S(1)} collective-permute-done((f32[7,8,16,8]{3,2,1,0:T(8,128)S(1)}, f32[7,8,16,8]{3,2,1,0:T(8,128)S(1)}, u32[]{:S(2)}, u32[]{:S(2)}) %collective-permute-start) | collective-permute-done | bytes 28704 | tf_op jit(solution)/shard_map/ppermute | solution.py:21
  44.8 1.4 pad_maximum_fusion.3
  46.3 1.9 collective-permute-start.3
  48.2 2.4 collective-permute-start.2
  50.6 3.6 %collective-permute-done.3 = f32[7,8,8,144]{3,2,1,0:T(8,128)S(1)} collective-permute-done((f32[7,8,8,144]{3,2,1,0:T(8,128)S(1)}, f32[7,8,8,144]{3,2,1,0:T(8,128)S(1)}, u32[]{:S(2)}, u32[]{:S(2)}) %collective-permute-start.3) | collective-permute-done | bytes 258080 | tf_op jit(solution)/shard_map/ppermute | solution.py:23
  54.2 3.8 %collective-permute-done.2 = f32[7,8,8,144]{3,2,1,0:T(8,128)S(1)} collective-permute-done((f32[7,8,8,144]{3,2,1,0:T(8,128)S(1)}, f32[7,8,8,144]{3,2,1,0:T(8,128)S(1)}, u32[]{:S(2)}, u32[]{:S(2)}) %collective-permute-start.2) | collective-permute-done | bytes 258080 | tf_op jit(solution)/shard_map/ppermute | solution.py:21
  58.5 1.3 collective-permute-start.5
  59.8 4.8 %collective-permute-start.4 = (f32[7,8,32,144]{3,2,1,0:T(8,128)S(1)}, f32[7,8,32,144]{3,2,1,0:T(8,128)S(1)}, u32[]{:S(2)}, u32[]{:S(2)}) collective-permute-start(f32[7,8,32,144]{3,2,1,0:T(8,128)S(1)} %pad_maximum_fusion.1), channel_id=1, source_target_pairs={{0,1},{2,3},{4,5},{6,7},{8,9},{10,11},{12,13},{14,15},{16,17},{18,... | collective-permute-start | bytes 3096584 | tf_op jit(solution)/shard_map/ppermute | solution.py:21
  64.5 36.9 %collective-permute-done.5 = f32[7,8,32,144]{3,2,1,0:T(8,128)S(1)} collective-permute-done((f32[7,8,32,144]{3,2,1,0:T(8,128)S(1)}, f32[7,8,32,144]{3,2,1,0:T(8,128)S(1)}, u32[]{:S(2)}, u32[]{:S(2)}) %collective-permute-start.5) | collective-permute-done | bytes 1032224 | tf_op jit(solution)/shard_map/ppermute | solution.py:23
  101.5 1.3 collective-permute-done.4
  102.8 4.7 %fusion = f32[7,24,32,128]{3,2,1,0:T(8,128)S(1)} fusion(f32[7,8,32,144]{3,2,1,0:T(8,128)S(1)} %collective-permute-done.5, f32[7,8,8,144]{3,2,1,0:T(8,128)S(1)} %collective-permute-done.3, f32[7,8,16,8]{3,2,1,0:T(8,128)S(1)} %collective-permute-done.1, f32[3,8,16,128]{3,2,1,0:T(8,128)S(1)} %slice_multiply_fusion.5, f32[4,8,16,128]{3,2,1,0:T(8,128)S(1)} %copy-done, ...), kind=kOutput, calls=%fused_computation | convolution fusion | flops 1195444224 | bytes 5849088 | tf_op jit(solution)/shard_map/fswz,zk->fswk/dot_general | solution.py:44
  107.5 1.5 fusion.61
  109.0 1.2 fusion.24
  110.5 1.9 collective-permute-start.13
  112.4 3.9 %collective-permute-start.12 = (f32[7,8,16,8]{3,1,2,0:T(8,128)S(1)}, f32[7,8,16,8]{3,1,2,0:T(8,128)S(1)}, u32[]{:S(2)}, u32[]{:S(2)}) collective-permute-start(f32[7,8,16,8]{3,1,2,0:T(8,128)S(1)} %get-tuple-element.33), channel_id=1, source_target_pairs={{0,32},{32,64},{64,96},{96,128},{128,160},{160,192},{192,224},{224... | collective-permute-start | bytes 86024 | tf_op jit(solution)/shard_map/ppermute | solution.py:21
  116.3 14.1 %collective-permute-done.13 = f32[7,8,16,8]{3,1,2,0:T(8,128)S(1)} collective-permute-done((f32[7,8,16,8]{3,1,2,0:T(8,128)S(1)}, f32[7,8,16,8]{3,1,2,0:T(8,128)S(1)}, u32[]{:S(2)}, u32[]{:S(2)}) %collective-permute-start.13) | collective-permute-done | bytes 28704 | tf_op jit(solution)/shard_map/ppermute | solution.py:23
  130.4 8.3 %collective-permute-done.12 = f32[7,8,16,8]{3,1,2,0:T(8,128)S(1)} collective-permute-done((f32[7,8,16,8]{3,1,2,0:T(8,128)S(1)}, f32[7,8,16,8]{3,1,2,0:T(8,128)S(1)}, u32[]{:S(2)}, u32[]{:S(2)}) %collective-permute-start.12) | collective-permute-done | bytes 28704 | tf_op jit(solution)/shard_map/ppermute | solution.py:21
  139.3 1.9 collective-permute-start.15
  141.2 2.4 collective-permute-start.14
  143.6 3.6 %collective-permute-done.15 = f32[7,8,8,144]{3,1,2,0:T(8,128)S(1)} collective-permute-done((f32[7,8,8,144]{3,1,2,0:T(8,128)S(1)}, f32[7,8,8,144]{3,1,2,0:T(8,128)S(1)}, u32[]{:S(2)}, u32[]{:S(2)}) %collective-permute-start.15) | collective-permute-done | bytes 258080 | tf_op jit(solution)/shard_map/ppermute | solution.py:23
  147.2 3.8 %collective-permute-done.14 = f32[7,8,8,144]{3,1,2,0:T(8,128)S(1)} collective-permute-done((f32[7,8,8,144]{3,1,2,0:T(8,128)S(1)}, f32[7,8,8,144]{3,1,2,0:T(8,128)S(1)}, u32[]{:S(2)}, u32[]{:S(2)}) %collective-permute-start.14) | collective-permute-done | bytes 258080 | tf_op jit(solution)/shard_map/ppermute | solution.py:21
  151.4 1.3 collective-permute-start.17
  152.7 4.8 %collective-permute-start.16 = (f32[7,8,32,144]{3,1,2,0:T(8,128)S(1)}, f32[7,8,32,144]{3,1,2,0:T(8,128)S(1)}, u32[]{:S(2)}, u32[]{:S(2)}) collective-permute-start(f32[7,8,32,144]{3,1,2,0:T(8,128)S(1)} %pad_maximum_fusion.2), channel_id=1, source_target_pairs={{0,1},{2,3},{4,5},{6,7},{8,9},{10,11},{12,13},{14,15},{16,17},{18,... | collective-permute-start | bytes 3096584 | tf_op jit(solution)/shard_map/ppermute | solution.py:21
  157.5 3.3 %collective-permute-start.9 = (f32[4,8,1,128]{3,1,2,0:T(8,128)S(1)}, f32[4,8,1,128]{3,1,2,0:T(8,128)S(1)}, u32[]{:S(2)}, u32[]{:S(2)}) collective-permute-start(f32[4,8,1,128]{3,1,2,0:T(8,128)S(1)} %get-tuple-element.31), channel_id=1, source_target_pairs={{0,2},{2,4},{4,6},{6,8},{8,10},{10,12},{12,14},{14,16},{16,18},{18... | collective-permute-start | bytes 49160 | tf_op jit(solution)/shard_map/ppermute | solution.py:21
  160.8 2.5 collective-permute-start.8
  163.3 3.1 collective-permute-done.8
  166.5 1.3 collective-permute-start.11
  167.8 1.3 collective-permute-start.10
  169.2 1.9 collective-permute-start.7
  171.2 38.2 %collective-permute-done.7 = f32[4,8,16,1]{3,1,2,0:T(8,128)S(1)} collective-permute-done((f32[4,8,16,1]{3,1,2,0:T(8,128)S(1)}, f32[4,8,16,1]{3,1,2,0:T(8,128)S(1)}, u32[]{:S(2)}, u32[]{:S(2)}) %collective-permute-start.7) | collective-permute-done | bytes 2080 | tf_op jit(solution)/shard_map/ppermute | solution.py:21
  209.3 1.9 collective-permute-start.6
  211.2 8.4 %collective-permute-done.6 = f32[4,8,16,1]{3,1,2,0:T(8,128)S(1)} collective-permute-done((f32[4,8,16,1]{3,1,2,0:T(8,128)S(1)}, f32[4,8,16,1]{3,1,2,0:T(8,128)S(1)}, u32[]{:S(2)}, u32[]{:S(2)}) %collective-permute-start.6) | collective-permute-done | bytes 2080 | tf_op jit(solution)/shard_map/ppermute | solution.py:23
  220.1 2.6 pad_maximum_fusion
  222.7 5.8 %fusion.16 = f32[7,24,32,128]{3,2,1,0:T(8,128)S(1)} fusion(f32[7,24,32,144]{3,1,2,0:T(8,128)S(1)} %pad_maximum_fusion), kind=kOutput, calls=%fused_computation.17 | convolution fusion | flops 1190025216 | bytes 5849088 | tf_op jit(solution)/shard_map/fswz,zk->fswk/dot_general | solution.py:44
  228.5 1.5 fusion.59
  230.0 1.2 fusion.27
  231.2 0.5 multiply_reduce_fusion
  231.8 81.2 %all-reduce = (f32[3,16]{1,0:T(4,128)S(1)}, f32[3,16]{1,0:T(4,128)S(1)}, f32[3,16]{1,0:T(4,128)S(1)}, f32[3,16]{1,0:T(4,128)S(1)}, f32[3,16]{1,0:T(4,128)S(1)}) all-reduce(f32[3,16]{1,0:T(4,128)S(1)} %get-tuple-element.11, f32[3,16]{1,0:T(4,128)S(1)} %get-tuple-element.12, ...), channel_id=1, replica_groups=mesh['span'=16,'wall'=16,'stream'=2] {'span'}, use_global_device_ids=true, to_apply=%region_1.2 | all-reduce | flops 240 | bytes 1920 | tf_op jit(solution)/shard_map/psum | solution.py:91
  313.0 6.7 %all-reduce.1 = (f32[3,16]{1,0:T(4,128)S(1)}, f32[3,16]{1,0:T(4,128)S(1)}, f32[3,16]{1,0:T(4,128)S(1)}, f32[3,16]{1,0:T(4,128)S(1)}, f32[3,16]{1,0:T(4,128)S(1)}) all-reduce(f32[3,16]{1,0:T(4,128)S(1)} %get-tuple-element.13, f32[3,16]{1,0:T(4,128)S(1)} %get-tuple-element.14, ...), channel_id=1, replica_groups=mesh['span'=16,'wall'=16,'stream'=2] {'stream'}, use_global_device_ids=true, to_apply=%region_2.3 | all-reduce | flops 240 | bytes 1920 | tf_op jit(solution)/shard_map/psum | solution.py:90
  319.7 0.6 rsqrt_multiply_fusion
  320.4 0.7 copy.5
  321.2 0.7 copy.6
  (25 shorter events, 2.5 us)
Async XLA Ops:
  2.4 55.6 %copy-start = (f32[4,8,16,128]{3,2,1,0:T(8,128)S(1)}, f32[4,8,16,128]{3,2,1,0:T(8,128)}, u32[]{:S(2)}) copy-start(f32[4,8,16,128]{3,2,1,0:T(8,128)} %param.1) | copy-start | bytes 786436
  3.7 32.7 %collective-permute-start.1 = (f32[7,8,16,8]{3,2,1,0:T(8,128)S(1)}, f32[7,8,16,8]{3,2,1,0:T(8,128)S(1)}, u32[]{:S(2)}, u32[]{:S(2)}) collective-permute-start(f32[7,8,16,8]{3,2,1,0:T(8,128)S(1)} %get-tuple-element.36), channel_id=1, source_target_pairs={{32,0},{64,32},{96,64},{128,96},{160,128},{192,160},{224,192},{256... | collective-permute-start | bytes 86024 | tf_op jit(solution)/shard_map/ppermute | solution.py:23
  16.9 27.9 %collective-permute-start = (f32[7,8,16,8]{3,2,1,0:T(8,128)S(1)}, f32[7,8,16,8]{3,2,1,0:T(8,128)S(1)}, u32[]{:S(2)}, u32[]{:S(2)}) collective-permute-start(f32[7,8,16,8]{3,2,1,0:T(8,128)S(1)} %get-tuple-element.35), channel_id=1, source_target_pairs={{0,32},{32,64},{64,96},{96,128},{128,160},{160,192},{192,224},{224... | collective-permute-start | bytes 86024 | tf_op jit(solution)/shard_map/ppermute | solution.py:21
  46.3 7.9 %collective-permute-start.3 = (f32[7,8,8,144]{3,2,1,0:T(8,128)S(1)}, f32[7,8,8,144]{3,2,1,0:T(8,128)S(1)}, u32[]{:S(2)}, u32[]{:S(2)}) collective-permute-start(f32[7,8,8,144]{3,2,1,0:T(8,128)S(1)} %get-tuple-element.28), channel_id=1, source_target_pairs={{2,0},{4,2},{6,4},{8,6},{10,8},{12,10},{14,12},{16,14},{18,16},{20... | collective-permute-start | bytes 774152 | tf_op jit(solution)/shard_map/ppermute | solution.py:23
  48.2 9.8 %collective-permute-start.2 = (f32[7,8,8,144]{3,2,1,0:T(8,128)S(1)}, f32[7,8,8,144]{3,2,1,0:T(8,128)S(1)}, u32[]{:S(2)}, u32[]{:S(2)}) collective-permute-start(f32[7,8,8,144]{3,2,1,0:T(8,128)S(1)} %get-tuple-element.27), channel_id=1, source_target_pairs={{0,2},{2,4},{4,6},{6,8},{8,10},{10,12},{12,14},{14,16},{16,18},{18... | collective-permute-start | bytes 774152 | tf_op jit(solution)/shard_map/ppermute | solution.py:21
  58.5 43.0 %collective-permute-start.5 = (f32[7,8,32,144]{3,2,1,0:T(8,128)S(1)}, f32[7,8,32,144]{3,2,1,0:T(8,128)S(1)}, u32[]{:S(2)}, u32[]{:S(2)}) collective-permute-start(f32[7,8,32,144]{3,2,1,0:T(8,128)S(1)} %pad_maximum_fusion.1), channel_id=1, source_target_pairs={{1,0},{3,2},{5,4},{7,6},{9,8},{11,10},{13,12},{15,14},{17,16},{19,... | collective-permute-start | bytes 3096584 | tf_op jit(solution)/shard_map/ppermute | solution.py:23
  59.8 43.0 %collective-permute-start.4 = (f32[7,8,32,144]{3,2,1,0:T(8,128)S(1)}, f32[7,8,32,144]{3,2,1,0:T(8,128)S(1)}, u32[]{:S(2)}, u32[]{:S(2)}) collective-permute-start(f32[7,8,32,144]{3,2,1,0:T(8,128)S(1)} %pad_maximum_fusion.1), channel_id=1, source_target_pairs={{0,1},{2,3},{4,5},{6,7},{8,9},{10,11},{12,13},{14,15},{16,17},{18,... | collective-permute-start | bytes 3096584 | tf_op jit(solution)/shard_map/ppermute | solution.py:21
  110.5 20.0 %collective-permute-start.13 = (f32[7,8,16,8]{3,1,2,0:T(8,128)S(1)}, f32[7,8,16,8]{3,1,2,0:T(8,128)S(1)}, u32[]{:S(2)}, u32[]{:S(2)}) collective-permute-start(f32[7,8,16,8]{3,1,2,0:T(8,128)S(1)} %get-tuple-element.34), channel_id=1, source_target_pairs={{32,0},{64,32},{96,64},{128,96},{160,128},{192,160},{224,192},{256... | collective-permute-start | bytes 86024 | tf_op jit(solution)/shard_map/ppermute | solution.py:23
  112.4 26.4 %collective-permute-start.12 = (f32[7,8,16,8]{3,1,2,0:T(8,128)S(1)}, f32[7,8,16,8]{3,1,2,0:T(8,128)S(1)}, u32[]{:S(2)}, u32[]{:S(2)}) collective-permute-start(f32[7,8,16,8]{3,1,2,0:T(8,128)S(1)} %get-tuple-element.33), channel_id=1, source_target_pairs={{0,32},{32,64},{64,96},{96,128},{128,160},{160,192},{192,224},{224... | collective-permute-start | bytes 86024 | tf_op jit(solution)/shard_map/ppermute | solution.py:21
  139.3 7.9 %collective-permute-start.15 = (f32[7,8,8,144]{3,1,2,0:T(8,128)S(1)}, f32[7,8,8,144]{3,1,2,0:T(8,128)S(1)}, u32[]{:S(2)}, u32[]{:S(2)}) collective-permute-start(f32[7,8,8,144]{3,1,2,0:T(8,128)S(1)} %get-tuple-element.26), channel_id=1, source_target_pairs={{2,0},{4,2},{6,4},{8,6},{10,8},{12,10},{14,12},{16,14},{18,16},{20... | collective-permute-start | bytes 774152 | tf_op jit(solution)/shard_map/ppermute | solution.py:23
  141.2 9.8 %collective-permute-start.14 = (f32[7,8,8,144]{3,1,2,0:T(8,128)S(1)}, f32[7,8,8,144]{3,1,2,0:T(8,128)S(1)}, u32[]{:S(2)}, u32[]{:S(2)}) collective-permute-start(f32[7,8,8,144]{3,1,2,0:T(8,128)S(1)} %get-tuple-element.25), channel_id=1, source_target_pairs={{0,2},{2,4},{4,6},{6,8},{8,10},{10,12},{12,14},{14,16},{16,18},{18... | collective-permute-start | bytes 774152 | tf_op jit(solution)/shard_map/ppermute | solution.py:21
  151.4 68.6 %collective-permute-start.17 = (f32[7,8,32,144]{3,1,2,0:T(8,128)S(1)}, f32[7,8,32,144]{3,1,2,0:T(8,128)S(1)}, u32[]{:S(2)}, u32[]{:S(2)}) collective-permute-start(f32[7,8,32,144]{3,1,2,0:T(8,128)S(1)} %pad_maximum_fusion.2), channel_id=1, source_target_pairs={{1,0},{3,2},{5,4},{7,6},{9,8},{11,10},{13,12},{15,14},{17,16},{19,... | collective-permute-start | bytes 3096584 | tf_op jit(solution)/shard_map/ppermute | solution.py:23
  152.7 67.3 %collective-permute-start.16 = (f32[7,8,32,144]{3,1,2,0:T(8,128)S(1)}, f32[7,8,32,144]{3,1,2,0:T(8,128)S(1)}, u32[]{:S(2)}, u32[]{:S(2)}) collective-permute-start(f32[7,8,32,144]{3,1,2,0:T(8,128)S(1)} %pad_maximum_fusion.2), channel_id=1, source_target_pairs={{0,1},{2,3},{4,5},{6,7},{8,9},{10,11},{12,13},{14,15},{16,17},{18,... | collective-permute-start | bytes 3096584 | tf_op jit(solution)/shard_map/ppermute | solution.py:21
  157.5 5.8 %collective-permute-start.9 = (f32[4,8,1,128]{3,1,2,0:T(8,128)S(1)}, f32[4,8,1,128]{3,1,2,0:T(8,128)S(1)}, u32[]{:S(2)}, u32[]{:S(2)}) collective-permute-start(f32[4,8,1,128]{3,1,2,0:T(8,128)S(1)} %get-tuple-element.31), channel_id=1, source_target_pairs={{0,2},{2,4},{4,6},{6,8},{8,10},{10,12},{12,14},{14,16},{16,18},{18... | collective-permute-start | bytes 49160 | tf_op jit(solution)/shard_map/ppermute | solution.py:21
  160.8 5.6 %collective-permute-start.8 = (f32[4,8,1,128]{3,1,2,0:T(8,128)S(1)}, f32[4,8,1,128]{3,1,2,0:T(8,128)S(1)}, u32[]{:S(2)}, u32[]{:S(2)}) collective-permute-start(f32[4,8,1,128]{3,1,2,0:T(8,128)S(1)} %get-tuple-element.32), channel_id=1, source_target_pairs={{2,0},{4,2},{6,4},{8,6},{10,8},{12,10},{14,12},{16,14},{18,16},{20... | collective-permute-start | bytes 49160 | tf_op jit(solution)/shard_map/ppermute | solution.py:23
  166.5 53.2 %collective-permute-start.11 = (f32[4,1,18,128]{3,1,2,0:T(1,128)S(1)}, f32[4,1,18,128]{3,1,2,0:T(1,128)S(1)}, u32[]{:S(2)}, u32[]{:S(2)}) collective-permute-start(f32[4,1,18,128]{3,1,2,0:T(1,128)S(1)} %get-tuple-element.40), channel_id=1, source_target_pairs={{0,1},{2,3},{4,5},{6,7},{8,9},{10,11},{12,13},{14,15},{16,17},{18,... | collective-permute-start | bytes 110600 | tf_op jit(solution)/shard_map/ppermute | solution.py:21
  167.8 51.9 %collective-permute-start.10 = (f32[4,1,18,128]{3,1,2,0:T(1,128)S(1)}, f32[4,1,18,128]{3,1,2,0:T(1,128)S(1)}, u32[]{:S(2)}, u32[]{:S(2)}) collective-permute-start(f32[4,1,18,128]{3,1,2,0:T(1,128)S(1)} %get-tuple-element.39), channel_id=1, source_target_pairs={{1,0},{3,2},{5,4},{7,6},{9,8},{11,10},{13,12},{15,14},{17,16},{19,... | collective-permute-start | bytes 110600 | tf_op jit(solution)/shard_map/ppermute | solution.py:23
  169.2 40.1 %collective-permute-start.7 = (f32[4,8,16,1]{3,1,2,0:T(8,128)S(1)}, f32[4,8,16,1]{3,1,2,0:T(8,128)S(1)}, u32[]{:S(2)}, u32[]{:S(2)}) collective-permute-start(f32[4,8,16,1]{3,1,2,0:T(8,128)S(1)} %get-tuple-element.30), channel_id=1, source_target_pairs={{0,32},{32,64},{64,96},{96,128},{128,160},{160,192},{192,224},{224... | collective-permute-start | bytes 6152 | tf_op jit(solution)/shard_map/ppermute | solution.py:21
  209.3 10.3 %collective-permute-start.6 = (f32[4,8,16,1]{3,1,2,0:T(8,128)S(1)}, f32[4,8,16,1]{3,1,2,0:T(8,128)S(1)}, u32[]{:S(2)}, u32[]{:S(2)}) collective-permute-start(f32[4,8,16,1]{3,1,2,0:T(8,128)S(1)} %get-tuple-element.29), channel_id=1, source_target_pairs={{32,0},{64,32},{96,64},{128,96},{160,128},{192,160},{224,192},{256... | collective-permute-start | bytes 6152 | tf_op jit(solution)/shard_map/ppermute | solution.py:23
